TPU v7x, 32 devices: a whole 2x2x4 slice. The times are simulated.
32 devices in a mesh: blk: 8 (over z, x), rep: 4 (over y, core).
Axes of the slice: x: 2, y: 2, z: 4, core: 2. Of those that a mesh axis runs over, the one named last changes fastest.
Arguments:
- features: bfloat16 [32768, 128], P('blk'), may hold values from -6 to 6
- weight: bfloat16 [128, 256], replicated, may hold values from -0.5 to 0.5
- bias: float32 [256], replicated, may hold values from -3 to 3
- tile_values: bfloat16 [8, 8, 160, 128, 128], P('blk', 'rep'), may hold values from 0 to 0.041748047
- tile_place: int32 [8, 8, 160], P('blk', 'rep'), may hold values from 0 to 1023, as said below
- tile_count: int32 [8, 8], P('blk', 'rep'), may hold values from 1 to 160, as said below
Outputs:
- activations: bfloat16 [32768, 256], P('blk')
Inputs may be any that keep to these rules, and one draw needn't show every extreme that they name: `tile_place`: within one pair of destination block and section the 160 positions are distinct. `tile_count`: some pair of destination block and section has all 160 slots occupied.
All inputs are finite; a program needn't handle non-finite values.
Results may differ from a plain program's by a relative error of at most 0.0046.
Values may be sent and summed in bfloat16 or wider, within the bound.
A program may use at most 128 MiB of HBM per device.

v0:
```python
import jax
import jax.numpy as jnp
from jax import lax
from jax.sharding import PartitionSpec as P

TILE = 128


def section_terms(source, tiles, place, count):
    row_count = source.shape[0]
    row_tiles = row_count // TILE
    column = place % row_tiles
    target = place // row_tiles
    blocked = source.reshape(row_tiles, TILE, source.shape[1])
    pieces = jnp.take(blocked, column, axis=0)
    products = jnp.einsum("kij,kjf->kif", tiles, pieces, preferred_element_type=jnp.float32)
    slot_ids = jnp.arange(place.shape[0], dtype=jnp.int32)
    live = (slot_ids < count).astype(jnp.float32)
    products = products * live[:, None, None]
    summed = jax.ops.segment_sum(products, target, num_segments=row_tiles)
    return summed.reshape(row_count, source.shape[1])


def shards(features, weight, bias, tile_values, tile_place, tile_count):
    row_count = features.shape[0]
    sections = tile_values.shape[1]
    cycle_size = lax.axis_size("blk")
    my_replica = lax.axis_index("rep")
    partial_value = jnp.zeros((row_count, features.shape[1]), jnp.float32)
    piece_rows = row_count // cycle_size
    pieces = features.reshape(cycle_size, piece_rows, features.shape[1])
    holding = lax.all_to_all(pieces, "blk", split_axis=0, concat_axis=0, tiled=True)
    for section_index in range(sections):
        offset = my_replica * sections + section_index
        rolled = jnp.roll(holding, offset, axis=0)
        arrived = lax.all_to_all(rolled, "blk", split_axis=0, concat_axis=0, tiled=True)
        source = arrived.reshape(row_count, features.shape[1])
        partial_value = partial_value + section_terms(
            source,
            tile_values[0, section_index],
            tile_place[0, section_index],
            tile_count[0, section_index],
        )
    summed = lax.psum(partial_value, "rep")
    aggregated = summed.astype(jnp.bfloat16)
    output = jnp.dot(aggregated, weight, preferred_element_type=jnp.float32) + bias
    return jnp.maximum(output, 0.0).astype(jnp.bfloat16)


def solution(mesh):
    in_specs = (
        P("blk", None),
        P(),
        P(),
        P("blk", "rep", None, None, None),
        P("blk", "rep", None),
        P("blk", "rep"),
    )
    out_specs = P("blk", None)
    return jax.shard_map(shards, mesh=mesh, in_specs=in_specs, out_specs=out_specs, check_vma=False)
```

profile of v0, /device:TPU:27, one launch (start us, length us, event | category | flops | bytes accessed | tf_op | source)
XLA Modules:
  0.0 221.2 jit_solution(2415213686946378558)
XLA Ops:
  0.0 0.0 copy-start
  0.0 5.6 %all-to-all-start = ((bf16[8,512,128]{2,1,0:T(8,128)(2,1)}), bf16[8,512,128]{2,1,0:T(8,128)(2,1)S(1)}, u32[]{:S(2)}, u32[]{:S(2)}) async-start(bf16[8,512,128]{2,1,0:T(8,128)(2,1)} %bitcast.45), calls=%async_computation | async-start | bytes 2097152 | tf_op jit(solution)/shard_map/all_to_all | solution.py:32
  5.6 24.1 %all-to-all-done = bf16[8,512,128]{2,1,0:T(8,128)(2,1)S(1)} async-done(((bf16[8,512,128]{2,1,0:T(8,128)(2,1)}), bf16[8,512,128]{2,1,0:T(8,128)(2,1)S(1)}, u32[]{:S(2)}, u32[]{:S(2)}) %all-to-all-start) | async-done | bytes 1048608 | tf_op jit(solution)/shard_map/all_to_all | solution.py:32
  29.7 0.1 constant_dynamic-update-slice_fusion.1
  29.8 0.0 copy-start.2
  29.8 0.0 copy-start.3
  29.8 0.1 constant_dynamic-update-slice_fusion
  29.9 1.1 constant_dynamic-slice_fusion
  31.1 28.8 %all_to_all.15 = bf16[8,512,128]{2,1,0:T(8,128)(2,1)S(1)} all-to-all(bf16[8,512,128]{2,1,0:T(8,128)(2,1)S(1)} %get-tuple-element.11), channel_id=1, replica_groups=mesh['blk'=8,'rep'=4] {'blk'}, dimensions={0} | all-to-all | bytes 2097152 | tf_op jit(solution)/shard_map/all_to_all | solution.py:36
  59.8 5.4 %all-to-all-start.1 = ((bf16[8,512,128]{2,1,0:T(8,128)(2,1)}), bf16[8,512,128]{2,1,0:T(8,128)(2,1)S(1)}, u32[]{:S(2)}, u32[]{:S(2)}) async-start(bf16[8,512,128]{2,1,0:T(8,128)(2,1)} %get-tuple-element.12), calls=%async_computation.1 | async-start | bytes 2097152 | tf_op jit(solution)/shard_map/all_to_all | solution.py:36
  65.3 0.0 copy-done.2
  65.3 0.0 copy-done.3
  65.3 0.7 fusion.28
  66.0 0.7 compare_and_fusion
  66.7 0.6 compare_and_fusion.1
  67.3 7.7 %gather_fusion.1 = bf16[160,128,128]{2,1,0:T(8,128)(2,1)} fusion(bf16[32,128,128]{2,1,0:T(8,128)(2,1)S(1)} %bitcast.43, s32[1024]{0:T(1024)S(1)} %pad_clamp_fusion), kind=kCustom, calls=%fused_computation.1.clone | custom fusion | bytes 10486400 | tf_op jit(solution)/shard_map/jit(_take)/gather | solution.py:15
  75.0 11.8 %multiply_bitcast_fusion = f32[160,128,128]{1,2,0:T(8,128)} fusion(f32[160]{0:T(256)S(1)} %get-tuple-element.20, bf16[1,2,160,128,128]{4,3,2,1,0:T(8,128)(2,1)} %param.13, bf16[160,128,128]{2,1,0:T(8,128)(2,1)} %gather_fusion.1, pred[160]{0:T(512)(128)(4,1)S(1)} %get-tuple-element.6), kind=kOutput, calls=%fused_computation.4 | convolution fusion | flops 676331520 | bytes 20972320 | tf_op jit(solution)/shard_map/kij,kjf->kif/dot_general | solution.py:16
  86.8 11.7 %copy.12 = f32[160,128,128]{2,1,0:T(8,128)} copy(f32[160,128,128]{1,2,0:T(8,128)} %multiply_bitcast_fusion) | data formatting | bytes 20971520 | tf_op jit(solution)/shard_map/mul | solution.py:19
  98.6 0.0 all-to-all-done.1
  98.6 7.7 %gather_fusion = bf16[160,128,128]{2,1,0:T(8,128)(2,1)} fusion(bf16[32,128,128]{2,1,0:T(8,128)(2,1)S(1)} %bitcast.42, s32[1024]{0:T(1024)S(1)} %pad_clamp_fusion.1), kind=kCustom, calls=%fused_computation.clone | custom fusion | bytes 10486400 | tf_op jit(solution)/shard_map/jit(_take)/gather | solution.py:15
  106.3 11.8 %multiply_bitcast_fusion.1 = f32[160,128,128]{1,2,0:T(8,128)} fusion(f32[160]{0:T(256)S(1)} %get-tuple-element.19, bf16[1,2,160,128,128]{4,3,2,1,0:T(8,128)(2,1)} %param.13, bf16[160,128,128]{2,1,0:T(8,128)(2,1)} %gather_fusion, pred[160]{0:T(512)(128)(4,1)S(1)} %get-tuple-element.9), kind=kOutput, calls=%fused_computation.5 | convolution fusion | flops 676331520 | bytes 20972320 | tf_op jit(solution)/shard_map/kij,kjf->kif/dot_general | solution.py:16
  118.1 11.7 %copy.10 = f32[160,128,128]{2,1,0:T(8,128)} copy(f32[160,128,128]{1,2,0:T(8,128)} %multiply_bitcast_fusion.1) | data formatting | bytes 20971520 | tf_op jit(solution)/shard_map/mul | solution.py:19
  129.8 0.2 broadcast.127.clone.1
  130.1 21.2 %scatter_fusion.1 = f32[32,128,128]{2,1,0:T(8,128)S(1)} fusion(f32[32,128,128]{2,1,0:T(8,128)S(1)} %broadcast.127.clone.1, s32[160]{0:T(256)S(1)} %bitcast.47, f32[160,128,128]{2,1,0:T(8,128)} %copy.12), kind=kCustom, calls=%fused_computation.3 | custom fusion | flops 2621440 | bytes 31457920 | tf_op jit(solution)/shard_map/scatter-add | solution.py:20
  151.2 0.0 copy-start.1
  151.3 1.3 copy-done.1
  152.6 0.2 broadcast.127.clone
  152.8 21.2 %scatter_fusion = f32[32,128,128]{2,1,0:T(8,128)S(1)} fusion(f32[32,128,128]{2,1,0:T(8,128)S(1)} %broadcast.127.clone, s32[160]{0:T(256)S(1)} %bitcast.46, f32[160,128,128]{2,1,0:T(8,128)} %copy.10), kind=kCustom, calls=%fused_computation.2 | custom fusion | flops 2621440 | bytes 31457920 | tf_op jit(solution)/shard_map/scatter-add | solution.py:20
  174.0 0.0 copy-start.4
  174.0 3.2 %add.66 = f32[32,128,128]{2,1,0:T(8,128)} add(f32[32,128,128]{2,1,0:T(8,128)S(1)} %scatter_fusion, f32[32,128,128]{2,1,0:T(8,128)} %copy-done.1) | non-fusion elementwise | flops 524288 | bytes 6291456 | tf_op jit(solution)/shard_map/add | solution.py:38
  177.2 41.9 %all-reduce.1 = bf16[4096,128]{1,0:T(8,128)(2,1)S(1)} all-reduce(f32[4096,128]{1,0:T(8,128)} %bitcast.44), channel_id=1, replica_groups=mesh['blk'=8,'rep'=4] {'rep'}, use_global_device_ids=true, to_apply=%region_2.5 | all-reduce | flops 524288 | bytes 3145728 | tf_op jit(solution)/shard_map/psum | solution.py:44
  219.1 0.0 copy-done
  219.1 0.0 copy-done.4
  219.1 2.0 fusion.11
  (4 shorter events, 0.0 us)
Async XLA Ops:
  0.0 219.1 %copy-start = (bf16[128,256]{1,0:T(8,128)(2,1)S(1)}, bf16[128,256]{1,0:T(8,128)(2,1)}, u32[]{:S(2)}) copy-start(bf16[128,256]{1,0:T(8,128)(2,1)} %param.11) | copy-start | bytes 196612
  0.0 29.7 %all-to-all-start = ((bf16[8,512,128]{2,1,0:T(8,128)(2,1)}), bf16[8,512,128]{2,1,0:T(8,128)(2,1)S(1)}, u32[]{:S(2)}, u32[]{:S(2)}) async-start(bf16[8,512,128]{2,1,0:T(8,128)(2,1)} %bitcast.45), calls=%async_computation | async-start | bytes 2097152 | tf_op jit(solution)/shard_map/all_to_all | solution.py:32
  29.8 35.5 %copy-start.2 = (s32[1,2,160]{2,1,0:T(2,128)S(1)}, s32[1,2,160]{2,1,0:T(2,128)}, u32[]{:S(2)}) copy-start(s32[1,2,160]{2,1,0:T(2,128)} %param.14) | copy-start | bytes 3844
  29.8 35.5 %copy-start.3 = (s32[1,2]{1,0:T(1,128)S(1)}, s32[1,2]{1,0:T(1,128)}, u32[]{:S(2)}) copy-start(s32[1,2]{1,0:T(1,128)} %param.15) | copy-start | bytes 28
  59.8 38.7 %all-to-all-start.1 = ((bf16[8,512,128]{2,1,0:T(8,128)(2,1)}), bf16[8,512,128]{2,1,0:T(8,128)(2,1)S(1)}, u32[]{:S(2)}, u32[]{:S(2)}) async-start(bf16[8,512,128]{2,1,0:T(8,128)(2,1)} %get-tuple-element.12), calls=%async_computation.1 | async-start | bytes 2097152 | tf_op jit(solution)/shard_map/all_to_all | solution.py:36
  151.2 1.3 copy-start.1
  174.0 45.1 %copy-start.4 = (f32[256]{0:T(256)S(1)}, f32[256]{0:T(256)}, u32[]{:S(2)}) copy-start(f32[256]{0:T(256)} %param.12) | copy-start | bytes 3076
where the time goes:
time: 224 us; the launch traced here: 221 us
  blocking collectives  70.7 us (32%)
  other arithmetic  46.8 us (21%)
  local copies, waits for them, and re-layouts  42.7 us (19%)
  matrix products  25.7 us (11%)
  waiting for transfers between devices  24.1 us (11%)
  starting transfers between devices  11 us (5%)
    scatter-add x2, other arithmetic, section_terms(): summed = jax.ops.segment_sum(products, target, num_segments=row_tiles)  42.4 us
    psum x1, blocking collectives, shards(): summed = lax.psum(partial_value, 'rep')  41.9 us
    all_to_all x1, blocking collectives, shards(): lax.all_to_all(rolled, 'blk', split_axis=0, concat_axis=0, tiled=True)  28.8 us
    all_to_all x1, waiting for transfers between devices, shards(): lax.all_to_all(pieces, 'blk', split_axis=0, concat_axis=0, tiled=True)  24.1 us
    dot_general x2, matrix products, section_terms(): jnp.einsum('kij,kjf->kif', tiles, pieces, preferred_element_type=jnp.floa...  23.6 us
    mul x2, local copies, waits for them, and re-layouts, section_terms(): products = products * live[:, None, None]  23.5 us
    gather x2, local copies, waits for them, and re-layouts, section_terms(): pieces = jnp.take(blocked, column, axis=0)  15.4 us
    all_to_all x1, starting transfers between devices, shards(): lax.all_to_all(pieces, 'blk', split_axis=0, concat_axis=0, tiled=True)  5.57 us
  transfers between devices with their start and end apart: 2, of which 1 were waited for; matrix products, arithmetic and copies ran while one was open for 15% of the time, Pallas kernels for 0%

commit v1 on v0

v1 whole, which is shorter than its diff:
```python
import functools

import jax
import jax.numpy as jnp
from jax import lax
from jax.experimental import pallas as pl
from jax.experimental.pallas import tpu as pltpu
from jax.sharding import PartitionSpec as P

MESH = pl.DeviceIdType.MESH
GROUP = 8
BLOCK = 32
CHUNKS = 4


def largest_divisor(number, most):
    return max(d for d in range(1, most + 1) if number % d == 0)


def section_kernel(first, group, place_ref, count_ref, source_ref, tiles_ref, *rest):
    acc_in_ref, acc_ref = (None, rest[0]) if first else rest
    step = pl.program_id(0)
    slots, tile = tiles_ref.shape[2], tiles_ref.shape[3]
    row_tiles = source_ref.shape[0] // tile
    count = count_ref[0]
    base = step * slots

    @pl.when(step == 0)
    def _():
        acc_ref[...] = jnp.zeros_like(acc_ref) if first else acc_in_ref[...]

    def body(g, carry):
        products, targets = [], []
        for u in range(group):
            k = g * group + u
            place = place_ref[base + k]
            column = lax.rem(place, row_tiles)
            targets.append(lax.div(place, row_tiles))
            piece = source_ref[pl.ds(pl.multiple_of(column * tile, tile), tile), :]
            product = jnp.dot(tiles_ref[0, 0, k], piece, preferred_element_type=jnp.float32)
            products.append(jnp.where(base + k < count, product, 0.0))
        for target, product in zip(targets, products):
            rows = pl.ds(pl.multiple_of(target * tile, tile), tile)
            acc_ref[rows, :] += product
        return carry

    live = jnp.clip(count - base, 0, slots)
    lax.fori_loop(0, (live + group - 1) // group, body, 0)


def section_sum(acc, source, tile_values, place, count, section):
    slots, tile = tile_values.shape[2], tile_values.shape[3]
    rows, width = source.shape
    block = largest_divisor(slots, BLOCK)
    group = largest_divisor(block, GROUP)
    first = acc is None

    def tiles_map(step, place_ref, count_ref):
        return (0, section, jnp.minimum(step, jnp.maximum(count_ref[0] - 1, 0) // block), 0, 0)

    whole = pl.BlockSpec((rows, width), lambda step, *_: (0, 0))
    in_specs = [whole, pl.BlockSpec((1, 1, block, tile, tile), tiles_map)]
    args = [source, tile_values]
    if not first:
        in_specs.append(whole)
        args.append(acc)
    return pl.pallas_call(
        functools.partial(section_kernel, first, group),
        out_shape=jax.ShapeDtypeStruct((rows, width), jnp.float32),
        grid_spec=pltpu.PrefetchScalarGridSpec(
            num_scalar_prefetch=2, grid=(slots // block,), in_specs=in_specs, out_specs=whole
        ),
        cost_estimate=pl.CostEstimate(
            flops=2 * slots * tile * tile * width, bytes_accessed=slots * tile * tile * 2, transcendentals=0
        ),
        name="section_sum",
    )(place, count, *args)


def reduce_kernel(chips, chunks, part_ref, agg_ref, core_in, send_buf, recv_buf,
                  s1, r1, s2, r2, s3, r3, s4, r4):
    blk, rep = lax.axis_index("blk"), lax.axis_index("rep")
    core, chip = lax.rem(rep, 2), lax.div(rep, 2)
    rows = part_ref.shape[0]
    half = rows // 2
    size = half // chips // chunks
    other = chip * 2 + (1 - core)

    def peer(d):
        return lax.rem(chip + d, chips)

    def local(piece, ch):
        return pl.ds(pl.multiple_of((piece * chunks + ch) * size, size), size)

    def place(which, piece, ch):
        return pl.ds(pl.multiple_of(which * half + (piece * chunks + ch) * size, size), size)

    barrier = pltpu.get_barrier_semaphore()
    pl.semaphore_signal(barrier, inc=1, device_id=(blk, other), device_id_type=MESH)
    for d in range(1, chips):
        pl.semaphore_signal(barrier, inc=1, device_id=(blk, peer(d) * 2 + core), device_id_type=MESH)
    pl.semaphore_wait(barrier, chips)

    order = [(ch, d) for ch in range(chunks) for d in list(range(1, chips)) + [0]]
    stage1, stage2, stage3, stage4 = {}, {}, {}, {}
    for ch, d in order:
        copy = pltpu.make_async_remote_copy(
            src_ref=part_ref.at[place(1 - core, peer(d), ch)], dst_ref=core_in.at[local(peer(d), ch)],
            send_sem=s1.at[d, ch], recv_sem=r1.at[d, ch], device_id=(blk, other), device_id_type=MESH)
        copy.start()
        stage1[ch, d] = copy
    for ch, d in order:
        if d == 0:
            continue
        stage1[ch, d].wait_recv()
        total = part_ref[place(core, peer(d), ch), :] + core_in[local(peer(d), ch), :]
        send_buf[d - 1, ch] = total.astype(jnp.bfloat16)
        copy = pltpu.make_async_remote_copy(
            src_ref=send_buf.at[d - 1, ch], dst_ref=recv_buf.at[d - 1, ch],
            send_sem=s2.at[d, ch], recv_sem=r2.at[d, ch],
            device_id=(blk, peer(d) * 2 + core), device_id_type=MESH)
        copy.start()
        stage2[ch, d] = copy
    for ch in range(chunks):
        stage1[ch, 0].wait_recv()
        total = part_ref[place(core, chip, ch), :] + core_in[local(chip, ch), :]
        for d in range(1, chips):
            stage2[ch, d].wait_recv()
            total = total + recv_buf[d - 1, ch].astype(jnp.float32)
        mine = place(core, chip, ch)
        agg_ref[mine, :] = total.astype(jnp.bfloat16)
        for d in list(range(1, chips)) + [0]:
            target = other if d == 0 else peer(d) * 2 + core
            copy = pltpu.make_async_remote_copy(
                src_ref=agg_ref.at[mine], dst_ref=agg_ref.at[mine],
                send_sem=s3.at[d, ch], recv_sem=r3.at[d, ch],
                device_id=(blk, target), device_id_type=MESH)
            copy.start()
            stage3[ch, d] = copy
    for ch in range(chunks):
        for d in range(1, chips):
            stage3[ch, d].wait_recv()
            came = place(core, lax.rem(chip + chips - d, chips), ch)
            copy = pltpu.make_async_remote_copy(
                src_ref=agg_ref.at[came], dst_ref=agg_ref.at[came],
                send_sem=s4.at[d, ch], recv_sem=r4.at[d, ch],
                device_id=(blk, other), device_id_type=MESH)
            copy.start()
            stage4[ch, d] = copy
    for ch, d in order:
        stage1[ch, d].wait_send()
        stage3[ch, d].wait_send()
        if d == 0:
            stage3[ch, d].wait_recv()
        else:
            stage2[ch, d].wait_send()
            stage4[ch, d].wait()


def replica_sum(part, replicas):
    rows, width = part.shape
    chips = replicas // 2
    chunks = largest_divisor(rows // 2 // chips // 16, CHUNKS)
    size = rows // 2 // chips // chunks
    dma = pltpu.SemaphoreType.DMA((chips, chunks))
    vmem = pl.BlockSpec(memory_space=pltpu.VMEM)
    return pl.pallas_call(
        functools.partial(reduce_kernel, chips, chunks),
        out_shape=jax.ShapeDtypeStruct((rows, width), jnp.bfloat16),
        in_specs=[vmem],
        out_specs=vmem,
        scratch_shapes=[
            pltpu.VMEM((rows // 2, width), jnp.float32),
            pltpu.VMEM((chips - 1, chunks, size, width), jnp.bfloat16),
            pltpu.VMEM((chips - 1, chunks, size, width), jnp.bfloat16),
        ] + [dma] * 8,
        compiler_params=pltpu.CompilerParams(collective_id=0, has_side_effects=True),
        name="replica_sum",
    )(part)


def shards(blocks, replicas, features, weight, bias, tile_values, tile_place, tile_count):
    sections = tile_values.shape[1]
    sources = []
    for section in range(sections):
        pairs = [
            (b * replicas + r, (b + r * sections + section) % blocks * replicas + r)
            for b in range(blocks) for r in range(replicas)
        ]
        sources.append(lax.ppermute(features, ("blk", "rep"), pairs))
    part = None
    for section in range(sections):
        part = section_sum(part, sources[section], tile_values, tile_place[0, section],
                           tile_count[0, section][None], section)
    aggregated = replica_sum(part, replicas)
    output = jnp.dot(aggregated, weight, preferred_element_type=jnp.float32) + bias
    return jnp.maximum(output, 0.0).astype(jnp.bfloat16)


def solution(mesh):
    in_specs = (
        P("blk", None),
        P(),
        P(),
        P("blk", "rep", None, None, None),
        P("blk", "rep", None),
        P("blk", "rep"),
    )
    body = functools.partial(shards, mesh.shape["blk"], mesh.shape["rep"])
    return jax.shard_map(body, mesh=mesh, in_specs=in_specs, out_specs=P("blk", None), check_vma=False)
```

time: 224 us -> 106 us (0.47)
  blocking collectives: 70.7 us -> 0 us
  Pallas kernels: 0 us -> 70.6 us
  other arithmetic: 46.8 us -> 0 us
  local copies, waits for them, and re-layouts: 42.7 us -> 4.62 us
  matrix products: 25.7 us -> 3.24 us
  starting transfers between devices: 11 us -> 3.4 us
    pallas_call x0 -> x3, Pallas kernels: none -> 70.6 us  [the longest x1 57.7 us: replica_sum(): pl.pallas_call(functools.partial(reduce_kernel, chips, chunks), out_shape...]
    scatter-add x2 -> x0, other arithmetic: 42.4 us -> none  [section_terms(): summed = jax.ops.segment_sum(products, target, num_segments=row_tiles)]
    psum x1 -> x0, blocking collectives: 41.9 us -> none  [shards(): summed = lax.psum(partial_value, 'rep')]
    all_to_all x1 -> x0, blocking collectives: 28.8 us -> none  [shards(): lax.all_to_all(rolled, 'blk', split_axis=0, concat_axis=0, tiled=True)]
    all_to_all x2 -> x0, waiting for transfers between devices: 24.1 us -> none  [the longest x1 24.1 us: shards(): lax.all_to_all(pieces, 'blk', split_axis=0, concat_axis=0, tiled=True)]
    dot_general x2 -> x0, matrix products: 23.6 us -> none  [section_terms(): jnp.einsum('kij,kjf->kif', tiles, pieces, preferred_element_type=jnp.floa...]
    mul x2 -> x0, local copies, waits for them, and re-layouts: 23.5 us -> none  [section_terms(): products = products * live[:, None, None]]
    ppermute x0 -> x2, waiting for transfers between devices: none -> 22.7 us  [shards(): sources.append(lax.ppermute(features, ('blk', 'rep'), pairs))]
  transfers between devices with their start and end apart: 2 -> 2, of which waited for: 1 -> 2; matrix products, arithmetic and copies ran while one was open for 15% -> 3% of each run, Pallas kernels for 0% -> 7%
where the time goes in v1:
time: 106 us; the launch traced here: 105 us
  Pallas kernels  70.6 us (67%)
  waiting for transfers between devices  22.7 us (21%)
  local copies, waits for them, and re-layouts  4.62 us (4%)
  starting transfers between devices  3.4 us (3%)
  matrix products  3.24 us (3%)
    pallas_call x1, Pallas kernels, replica_sum(): pl.pallas_call(functools.partial(reduce_kernel, chips, chunks), out_shape...  57.7 us
    ppermute x2, waiting for transfers between devices, shards(): sources.append(lax.ppermute(features, ('blk', 'rep'), pairs))  22.7 us
    pallas_call x2, Pallas kernels, section_sum(): pl.pallas_call(functools.partial(section_kernel, first, group), out_shape...  12.9 us
    ppermute x2, starting transfers between devices, shards(): sources.append(lax.ppermute(features, ('blk', 'rep'), pairs))  3.4 us
    dot_general x1, matrix products, shards(): jnp.dot(aggregated, weight, preferred_element_type=jnp.float32) + bias  3.24 us
  transfers between devices with their start and end apart: 2, of which 2 were waited for; matrix products, arithmetic and copies ran while one was open for 3% of the time, Pallas kernels for 7%

profile of v1, /device:TPU:27, one launch (start us, length us, event | category | flops | bytes accessed | tf_op | source)
XLA Modules:
  0.0 104.6 jit_solution(34833422308504953)
XLA Ops:
  0.0 0.0 copy-start
  0.0 2.0 %collective-permute-start.1 = (bf16[4096,128]{1,0:T(8,128)(2,1)}, bf16[4096,128]{1,0:T(8,128)(2,1)S(1)}, u32[]{:S(2)}, u32[]{:S(2)}) collective-permute-start(bf16[4096,128]{1,0:T(8,128)(2,1)} %param.6), channel_id=1, source_target_pairs={{0,0},{1,9},{2,18},{3,27},{4,4},{5,13},{6,22},{7,31},{8,8},{9,17},... | collective-permute-start | bytes 3145736 | tf_op jit(solution)/shard_map/ppermute | solution.py:190
  2.1 1.4 %collective-permute-start = (bf16[4096,128]{1,0:T(8,128)(2,1)}, bf16[4096,128]{1,0:T(8,128)(2,1)S(1)}, u32[]{:S(2)}, u32[]{:S(2)}) collective-permute-start(bf16[4096,128]{1,0:T(8,128)(2,1)} %param.6), channel_id=1, source_target_pairs={{0,4},{1,13},{2,22},{3,31},{4,8},{5,17},{6,26},{7,3},{8,12},{9,21}... | collective-permute-start | bytes 3145736 | tf_op jit(solution)/shard_map/ppermute | solution.py:190
  3.4 1.3 %fusion.3 = (s32[1,1]{1,0:T(1,128)}, s32[1,1]{1,0:T(1,128)}) fusion(s32[1,2]{1,0:T(1,128)} %param.11), kind=kLoop, calls=%fused_computation.4 | loop fusion | bytes 16 | tf_op jit(solution)/shard_map/slice | solution.py:194
  4.8 1.3 %fusion.2 = (s32[1,1,160]{2,1,0:T(1,128)}, s32[1,1,160]{2,1,0:T(1,128)}) fusion(s32[1,2,160]{2,1,0:T(2,128)} %param.10), kind=kLoop, calls=%fused_computation.3 | loop fusion | bytes 2560 | tf_op jit(solution)/shard_map/slice | solution.py:193
  6.1 20.2 %collective-permute-done.1.source_ref = bf16[4096,128]{1,0:T(8,128)(2,1)S(1)} collective-permute-done((bf16[4096,128]{1,0:T(8,128)(2,1)}, bf16[4096,128]{1,0:T(8,128)(2,1)S(1)}, u32[]{:S(2)}, u32[]{:S(2)}) %collective-permute-start.1) | collective-permute-done | bytes 1048608 | tf_op jit(solution)/shard_map/ppermute | solution.py:190
  26.3 0.0 copy-start.2
  26.3 1.0 copy-done.2
  27.3 6.9 %section_sum.2.rest_0_ = f32[4096,128]{1,0:T(8,128)} custom-call(s32[160]{0:T(256)} %bitcast.7, s32[1]{0:T(128)} %bitcast.3.count_ref, bf16[4096,128]{1,0:T(8,128)(2,1)} %copy-done.2, bf16[1,2,160,128,128]{4,3,2,1,0:T(8,128)(2,1)} %tiles_ref.3), custom_call_target="tpu_custom_call" | custom-call | flops 671088640 | bytes 5242880 | tf_op jit(solution)/shard_map/section_sum/pallas_call | solution.py:67
  34.1 2.5 %collective-permute-done.source_ref = bf16[4096,128]{1,0:T(8,128)(2,1)S(1)} collective-permute-done((bf16[4096,128]{1,0:T(8,128)(2,1)}, bf16[4096,128]{1,0:T(8,128)(2,1)S(1)}, u32[]{:S(2)}, u32[]{:S(2)}) %collective-permute-start) | collective-permute-done | bytes 1048608 | tf_op jit(solution)/shard_map/ppermute | solution.py:190
  36.6 0.0 copy-start.1
  36.6 1.0 copy-done.1
  37.6 0.0 copy-start.3
  37.6 6.0 %section_sum.3.part_ref = f32[4096,128]{1,0:T(8,128)} custom-call(s32[160]{0:T(256)} %bitcast.6, s32[1]{0:T(128)} %bitcast.1.count_ref, bf16[4096,128]{1,0:T(8,128)(2,1)} %copy-done.1, bf16[1,2,160,128,128]{4,3,2,1,0:T(8,128)(2,1)} %tiles_ref.3, f32[4096,128]{1,0:T(8,128)} %section_sum.2.rest_0_), custom_call_target="tpu_custom_call" | custom-call | flops 671088640 | bytes 5242880 | tf_op jit(solution)/shard_map/section_sum/pallas_call | solution.py:67
  43.6 57.7 %replica_sum.1 = bf16[4096,128]{1,0:T(8,128)(2,1)} custom-call(f32[4096,128]{1,0:T(8,128)} %section_sum.3.part_ref), custom_call_target="tpu_custom_call" | custom-call | tf_op jit(solution)/shard_map/replica_sum/pallas_call | solution.py:167
  101.3 0.0 copy-done
  101.3 0.0 copy-done.3
  101.3 3.2 %fusion.1 = bf16[4096,256]{1,0:T(8,128)(2,1)} fusion(bf16[4096,128]{1,0:T(8,128)(2,1)} %replica_sum.1, bf16[128,256]{1,0:T(8,128)(2,1)S(1)} %copy-done, f32[256]{0:T(256)S(1)} %copy-done.3), kind=kOutput, calls=%fused_computation.2 | convolution fusion | flops 271581184 | bytes 3212288 | tf_op jit(solution)/shard_map/dot_general | solution.py:196
Async XLA Ops:
  0.0 101.3 %copy-start = (bf16[128,256]{1,0:T(8,128)(2,1)S(1)}, bf16[128,256]{1,0:T(8,128)(2,1)}, u32[]{:S(2)}) copy-start(bf16[128,256]{1,0:T(8,128)(2,1)} %param.7) | copy-start | bytes 196612
  0.0 26.3 %collective-permute-start.1 = (bf16[4096,128]{1,0:T(8,128)(2,1)}, bf16[4096,128]{1,0:T(8,128)(2,1)S(1)}, u32[]{:S(2)}, u32[]{:S(2)}) collective-permute-start(bf16[4096,128]{1,0:T(8,128)(2,1)} %param.6), channel_id=1, source_target_pairs={{0,0},{1,9},{2,18},{3,27},{4,4},{5,13},{6,22},{7,31},{8,8},{9,17},... | collective-permute-start | bytes 3145736 | tf_op jit(solution)/shard_map/ppermute | solution.py:190
  2.1 34.6 %collective-permute-start = (bf16[4096,128]{1,0:T(8,128)(2,1)}, bf16[4096,128]{1,0:T(8,128)(2,1)S(1)}, u32[]{:S(2)}, u32[]{:S(2)}) collective-permute-start(bf16[4096,128]{1,0:T(8,128)(2,1)} %param.6), channel_id=1, source_target_pairs={{0,4},{1,13},{2,22},{3,31},{4,8},{5,17},{6,26},{7,3},{8,12},{9,21}... | collective-permute-start | bytes 3145736 | tf_op jit(solution)/shard_map/ppermute | solution.py:190
  26.3 1.0 copy-start.2
  36.6 1.0 copy-start.1
  37.6 63.7 %copy-start.3 = (f32[256]{0:T(256)S(1)}, f32[256]{0:T(256)}, u32[]{:S(2)}) copy-start(f32[256]{0:T(256)} %param.8) | copy-start | bytes 3076

commit v2 on v1

--- a/solution.py
+++ b/solution.py
@@ -17,26 +17,148 @@
     return max(d for d in range(1, most + 1) if number % d == 0)
 
 
-def section_kernel(first, group, place_ref, count_ref, source_ref, tiles_ref, *rest):
-    acc_in_ref, acc_ref = (None, rest[0]) if first else rest
+def gather_kernel(blocks, replicas, sections, features_ref, source_ref, ring,
+                  ring_send, ring_recv, give_send, give_recv, own_sem):
+    blk, rep = lax.axis_index("blk"), lax.axis_index("rep")
+    share = features_ref.shape[0] // replicas
+    sub = share // 2
+    odd = lax.rem(blk, 2)
+    position = (1 - odd) * lax.div(blk, 2) + odd * (blocks - 1 - lax.div(blk, 2))
+
+    def block_at(offset):
+        p = lax.rem(position + blocks + offset, blocks)
+        back = lax.div(p, blocks // 2)
+        return (1 - back) * (2 * p) + back * (2 * (blocks - 1 - p) + 1)
+
+    def rows(who, h):
+        return pl.ds(pl.multiple_of(who * share + h * sub, sub), sub)
+
+    hops = blocks // 2
+    ways = (1, -1)
+    barrier = pltpu.get_barrier_semaphore()
+    for way in ways:
+        pl.semaphore_signal(barrier, inc=1, device_id=(block_at(way), rep), device_id_type=MESH)
+    for d in range(1, replicas):
+        pl.semaphore_signal(barrier, inc=1, device_id=(blk, lax.rem(rep + d, replicas)), device_id_type=MESH)
+    pl.semaphore_wait(barrier, replicas + 1)
+
+    def ring_copy(w, k, h):
+        source = features_ref.at[rows(rep, h)] if k == 0 else ring.at[w, k - 1, h]
+        return pltpu.make_async_remote_copy(
+            src_ref=source, dst_ref=ring.at[w, k, h], send_sem=ring_send.at[w, k, h],
+            recv_sem=ring_recv.at[w, k, h], device_id=(block_at(ways[w]), rep), device_id_type=MESH)
+
+    def travels(w, k, h):
+        return k < hops - 1 or (k == hops - 1 and h == w)
+
+    for h in range(2):
+        for w in range(2):
+            if travels(w, 0, h):
+                ring_copy(w, 0, h).start()
+    own = pltpu.make_async_copy(features_ref, source_ref.at[0], own_sem)
+
+    @pl.when(rep == 0)
+    def _():
+        own.start()
+
+    arrivals = [(k, h, w) for k in range(hops) for h in range(2) for w in range(2) if travels(w, k, h)]
+
+    def give(k, h, w):
+        section = lax.rem(blk - block_at(-ways[w] * (k + 1)) + blocks, blocks)
+        target, index = lax.div(section, sections), lax.rem(section, sections)
+        place = source_ref.at[index, rows(rep, h)]
+        here = pltpu.make_async_copy(ring.at[w, k, h], place, give_send.at[w, k, h])
+        there = pltpu.make_async_remote_copy(
+            src_ref=ring.at[w, k, h], dst_ref=place, send_sem=give_send.at[w, k, h],
+            recv_sem=give_recv.at[index, rep, h], device_id=(blk, target), device_id_type=MESH)
+        return target, here, there
+
+    for k, h, w in arrivals:
+        ring_copy(w, k, h).wait_recv()
+        if travels(w, k + 1, h):
+            ring_copy(w, k + 1, h).start()
+        target, here, there = give(k, h, w)
+
+        @pl.when(target == rep)
+        def _():
+            here.start()
+
+        @pl.when(target != rep)
+        def _():
+            there.start()
+
+    for k, h, w in arrivals:
+        ring_copy(w, k, h).wait_send()
+        target, here, there = give(k, h, w)
+
+        @pl.when(target == rep)
+        def _():
+            here.wait()
+
+        @pl.when(target != rep)
+        def _():
+            there.wait_send()
+
+    @pl.when(rep == 0)
+    def _():
+        own.wait()
+
+    for index in range(sections):
+        def arrive(index=index):
+            for d in range(1, replicas):
+                giver = lax.rem(rep + d, replicas)
+                for h in range(2):
+                    pltpu.make_async_remote_copy(
+                        src_ref=ring.at[0, 0, h], dst_ref=source_ref.at[index, rows(giver, h)],
+                        send_sem=give_send.at[0, 0, h], recv_sem=give_recv.at[index, giver, h],
+                        device_id=(blk, giver), device_id_type=MESH).wait_recv()
+
+        if index == 0:
+            pl.when(rep != 0)(arrive)
+        else:
+            arrive()
+
+
+def gather_sources(features, blocks, replicas, sections):
+    rows, width = features.shape
+    sub = rows // replicas // 2
+    hops = blocks // 2
+    vmem = pl.BlockSpec(memory_space=pltpu.VMEM)
+    dma = pltpu.SemaphoreType.DMA
+    return pl.pallas_call(
+        functools.partial(gather_kernel, blocks, replicas, sections),
+        out_shape=jax.ShapeDtypeStruct((sections, rows, width), features.dtype),
+        in_specs=[vmem],
+        out_specs=vmem,
+        scratch_shapes=[
+            pltpu.VMEM((2, hops, 2, sub, width), features.dtype),
+            dma((2, hops, 2)), dma((2, hops, 2)), dma((2, hops, 2)), dma((sections, replicas, 2)), dma(()),
+        ],
+        compiler_params=pltpu.CompilerParams(collective_id=1, has_side_effects=True),
+        name="gather_sources",
+    )(features)
+
+
+def sections_kernel(find, group, place_ref, count_ref, source_ref, tiles_ref, acc_ref):
     step = pl.program_id(0)
     slots, tile = tiles_ref.shape[2], tiles_ref.shape[3]
-    row_tiles = source_ref.shape[0] // tile
-    count = count_ref[0]
-    base = step * slots
+    row_tiles = source_ref.shape[1] // tile
+    section, chunk, active = find(step, count_ref)
+    count = count_ref[0, section]
+    base = chunk * slots
 
     @pl.when(step == 0)
     def _():
-        acc_ref[...] = jnp.zeros_like(acc_ref) if first else acc_in_ref[...]
+        acc_ref[...] = jnp.zeros_like(acc_ref)
 
     def body(g, carry):
         products, targets = [], []
         for u in range(group):
             k = g * group + u
-            place = place_ref[base + k]
+            place = place_ref[0, section, base + k]
             column = lax.rem(place, row_tiles)
             targets.append(lax.div(place, row_tiles))
-            piece = source_ref[pl.ds(pl.multiple_of(column * tile, tile), tile), :]
+            piece = source_ref[section, pl.ds(pl.multiple_of(column * tile, tile), tile), :]
             product = jnp.dot(tiles_ref[0, 0, k], piece, preferred_element_type=jnp.float32)
             products.append(jnp.where(base + k < count, product, 0.0))
         for target, product in zip(targets, products):
@@ -44,37 +166,41 @@
             acc_ref[rows, :] += product
         return carry
 
-    live = jnp.clip(count - base, 0, slots)
+    live = jnp.where(active, jnp.clip(count - base, 0, slots), 0)
     lax.fori_loop(0, (live + group - 1) // group, body, 0)
 
 
-def section_sum(acc, source, tile_values, place, count, section):
-    slots, tile = tile_values.shape[2], tile_values.shape[3]
-    rows, width = source.shape
+def section_sums(sources, tile_values, tile_place, tile_count):
+    sections, slots, tile = tile_values.shape[1:4]
+    rows, width = sources.shape[1:]
     block = largest_divisor(slots, BLOCK)
     group = largest_divisor(block, GROUP)
-    first = acc is None
+
+    def find(step, count_ref):
+        section, chunk = jnp.int32(0), jnp.int32(0)
+        start, active = jnp.int32(0), False
+        for s in range(sections):
+            steps = lax.div(count_ref[0, s] + block - 1, block)
+            inside = step >= start
+            section = jnp.where(inside, s, section)
+            chunk = jnp.where(inside, jnp.minimum(step - start, steps - 1), chunk)
+            start = start + steps
+        return section, chunk, step < start
 
     def tiles_map(step, place_ref, count_ref):
-        return (0, section, jnp.minimum(step, jnp.maximum(count_ref[0] - 1, 0) // block), 0, 0)
-
-    whole = pl.BlockSpec((rows, width), lambda step, *_: (0, 0))
-    in_specs = [whole, pl.BlockSpec((1, 1, block, tile, tile), tiles_map)]
-    args = [source, tile_values]
-    if not first:
-        in_specs.append(whole)
-        args.append(acc)
+        section, chunk, _ = find(step, count_ref)
+        return (0, section, chunk, 0, 0)
+
+    vmem = pl.BlockSpec(memory_space=pltpu.VMEM)
     return pl.pallas_call(
-        functools.partial(section_kernel, first, group),
+        functools.partial(sections_kernel, find, group),
         out_shape=jax.ShapeDtypeStruct((rows, width), jnp.float32),
         grid_spec=pltpu.PrefetchScalarGridSpec(
-            num_scalar_prefetch=2, grid=(slots // block,), in_specs=in_specs, out_specs=whole
+            num_scalar_prefetch=2, grid=(sections * slots // block,),
+            in_specs=[vmem, pl.BlockSpec((1, 1, block, tile, tile), tiles_map)], out_specs=vmem
         ),
-        cost_estimate=pl.CostEstimate(
-            flops=2 * slots * tile * tile * width, bytes_accessed=slots * tile * tile * 2, transcendentals=0
-        ),
-        name="section_sum",
-    )(place, count, *args)
+        name="section_sums",
+    )(tile_place, tile_count, sources, tile_values)
 
 
 def reduce_kernel(chips, chunks, part_ref, agg_ref, core_in, send_buf, recv_buf,
@@ -180,18 +306,8 @@
 
 
 def shards(blocks, replicas, features, weight, bias, tile_values, tile_place, tile_count):
-    sections = tile_values.shape[1]
-    sources = []
-    for section in range(sections):
-        pairs = [
-            (b * replicas + r, (b + r * sections + section) % blocks * replicas + r)
-            for b in range(blocks) for r in range(replicas)
-        ]
-        sources.append(lax.ppermute(features, ("blk", "rep"), pairs))
-    part = None
-    for section in range(sections):
-        part = section_sum(part, sources[section], tile_values, tile_place[0, section],
-                           tile_count[0, section][None], section)
+    sources = gather_sources(features, blocks, replicas, tile_values.shape[1])
+    part = section_sums(sources, tile_values, tile_place, tile_count)
     aggregated = replica_sum(part, replicas)
     output = jnp.dot(aggregated, weight, preferred_element_type=jnp.float32) + bias
     return jnp.maximum(output, 0.0).astype(jnp.bfloat16)

time: 106 us -> 71.2 us (0.67); the launches traced: 105 us -> 71 us
  waiting for transfers between devices: 22.7 us -> 0 us
  local copies, waits for them, and re-layouts: 4.62 us -> 0.01 us
  starting transfers between devices: 3.4 us -> 0 us
  Pallas kernels: 70.6 us -> 67.7 us
    pallas_call x1, Pallas kernels: 57.7 us -> 18.2 us  [replica_sum(): pl.pallas_call(functools.partial(reduce_kernel, chips, chunks), out_shape...]
    pallas_call x2, Pallas kernels: 12.9 us -> 49.4 us  [the longest x1 36.6 us: gather_sources(): pl.pallas_call(functools.partial(gather_kernel, blocks, replicas, section...]
    ppermute x2 -> x0, waiting for transfers between devices: 22.7 us -> none  [shards(): sources.append(lax.ppermute(features, ('blk', 'rep'), pairs))]
    ppermute x2 -> x0, starting transfers between devices: 3.4 us -> none  [shards(): sources.append(lax.ppermute(features, ('blk', 'rep'), pairs))]
    slice x2 -> x0, local copies, waits for them, and re-layouts: 2.67 us -> none  [the longest x1 1.33 us: shards(): tile_count[0, section][None]]
    unnamed x8 -> x4, local copies, waits for them, and re-layouts: 1.96 us -> 0.01 us
  transfers between devices with their start and end apart: 2 -> 0, of which waited for: 2 -> 0; matrix products, arithmetic and copies ran while one was open for 3% -> 0% of each run, Pallas kernels for 7% -> 0%
where the time goes in v2:
time: 71.2 us; the launch traced here: 71 us
  Pallas kernels  67.7 us (95%)
  matrix products  3.24 us (5%)
    pallas_call x1, Pallas kernels, gather_sources(): pl.pallas_call(functools.partial(gather_kernel, blocks, replicas, section...  36.6 us
    pallas_call x1, Pallas kernels, replica_sum(): pl.pallas_call(functools.partial(reduce_kernel, chips, chunks), out_shape...  18.2 us
    pallas_call x1, Pallas kernels, section_sums(): pl.pallas_call(functools.partial(sections_kernel, find, group), out_shape...  12.8 us
    dot_general x1, matrix products, shards(): jnp.dot(aggregated, weight, preferred_element_type=jnp.float32) + bias  3.24 us

profile of v2, /device:TPU:27, one launch (start us, length us, event | category | flops | bytes accessed | tf_op | source)
XLA Modules:
  0.0 71.0 jit_solution(11805109214236969136)
XLA Ops:
  0.0 0.0 copy-start
  0.0 36.6 %gather_sources.1.source_ref = bf16[2,4096,128]{2,1,0:T(8,128)(2,1)} custom-call(bf16[4096,128]{1,0:T(8,128)(2,1)} %features_ref.1), custom_call_target="tpu_custom_call" | custom-call | tf_op jit(solution)/shard_map/gather_sources/pallas_call | solution.py:128
  36.6 0.0 copy-start.1
  36.6 12.8 %section_sums.1.part_ref = f32[4096,128]{1,0:T(8,128)} custom-call(s32[1,2,160]{2,1,0:T(2,128)} %place_ref.1, s32[1,2]{1,0:T(1,128)} %count_ref.1, bf16[2,4096,128]{2,1,0:T(8,128)(2,1)} %gather_sources.1.source_ref, bf16[1,2,160,128,128]{4,3,2,1,0:T(8,128)(2,1)} %tiles_ref.1), custom_call_target="tpu_custom_call" | custom-call | tf_op jit(solution)/shard_map/section_sums/pallas_call | solution.py:195
  49.4 18.2 %replica_sum.1 = bf16[4096,128]{1,0:T(8,128)(2,1)} custom-call(f32[4096,128]{1,0:T(8,128)} %section_sums.1.part_ref), custom_call_target="tpu_custom_call" | custom-call | tf_op jit(solution)/shard_map/replica_sum/pallas_call | solution.py:293
  67.7 0.0 copy-done
  67.7 0.0 copy-done.1
  67.7 3.2 %fusion.1 = bf16[4096,256]{1,0:T(8,128)(2,1)} fusion(bf16[4096,128]{1,0:T(8,128)(2,1)} %replica_sum.1, bf16[128,256]{1,0:T(8,128)(2,1)S(1)} %copy-done, f32[256]{0:T(256)S(1)} %copy-done.1), kind=kOutput, calls=%fused_computation.2 | convolution fusion | flops 271581184 | bytes 3212288 | tf_op jit(solution)/shard_map/dot_general | solution.py:312
Async XLA Ops:
  0.0 67.7 %copy-start = (bf16[128,256]{1,0:T(8,128)(2,1)S(1)}, bf16[128,256]{1,0:T(8,128)(2,1)}, u32[]{:S(2)}) copy-start(bf16[128,256]{1,0:T(8,128)(2,1)} %param.7) | copy-start | bytes 196612
  36.6 31.1 %copy-start.1 = (f32[256]{0:T(256)S(1)}, f32[256]{0:T(256)}, u32[]{:S(2)}) copy-start(f32[256]{0:T(256)} %param.8) | copy-start | bytes 3076

commit v3 on v2

--- a/solution.py
+++ b/solution.py
@@ -8,20 +8,23 @@
 from jax.sharding import PartitionSpec as P
 
 MESH = pl.DeviceIdType.MESH
-GROUP = 8
-BLOCK = 32
+GROUP = 16
+BLOCK = 80
 CHUNKS = 4
+SUBS = 4
+ROWS_STEP = 4096
+GRANT = 16 * 1024 * 1024
 
 
 def largest_divisor(number, most):
     return max(d for d in range(1, most + 1) if number % d == 0)
 
 
-def gather_kernel(blocks, replicas, sections, features_ref, source_ref, ring,
-                  ring_send, ring_recv, give_send, give_recv, own_sem):
+def gather_kernel(blocks, replicas, sections, subs, features_ref, tiles_ref, source_ref, held_ref, ring,
+                  ring_send, ring_recv, give_send, give_recv, own_sem, held_sem):
     blk, rep = lax.axis_index("blk"), lax.axis_index("rep")
     share = features_ref.shape[0] // replicas
-    sub = share // 2
+    sub = share // subs
     odd = lax.rem(blk, 2)
     position = (1 - odd) * lax.div(blk, 2) + odd * (blocks - 1 - lax.div(blk, 2))
 
@@ -49,19 +52,21 @@
             recv_sem=ring_recv.at[w, k, h], device_id=(block_at(ways[w]), rep), device_id_type=MESH)
 
     def travels(w, k, h):
-        return k < hops - 1 or (k == hops - 1 and h == w)
-
-    for h in range(2):
+        return k < hops - 1 or (k == hops - 1 and h * 2 // subs == w)
+
+    for h in range(subs):
         for w in range(2):
             if travels(w, 0, h):
                 ring_copy(w, 0, h).start()
+    held = pltpu.make_async_copy(tiles_ref, held_ref, held_sem)
+    held.start()
     own = pltpu.make_async_copy(features_ref, source_ref.at[0], own_sem)
 
     @pl.when(rep == 0)
     def _():
         own.start()
 
-    arrivals = [(k, h, w) for k in range(hops) for h in range(2) for w in range(2) if travels(w, k, h)]
+    arrivals = [(k, h, w) for k in range(hops) for h in range(subs) for w in range(2) if travels(w, k, h)]
 
     def give(k, h, w):
         section = lax.rem(blk - block_at(-ways[w] * (k + 1)) + blocks, blocks)
@@ -103,11 +108,12 @@
     def _():
         own.wait()
 
+    held.wait()
     for index in range(sections):
         def arrive(index=index):
             for d in range(1, replicas):
                 giver = lax.rem(rep + d, replicas)
-                for h in range(2):
+                for h in range(subs):
                     pltpu.make_async_remote_copy(
                         src_ref=ring.at[0, 0, h], dst_ref=source_ref.at[index, rows(giver, h)],
                         send_sem=give_send.at[0, 0, h], recv_sem=give_recv.at[index, giver, h],
@@ -119,24 +125,33 @@
             arrive()
 
 
-def gather_sources(features, blocks, replicas, sections):
+def gather_sources(features, tile_values, blocks, replicas):
+    sections = tile_values.shape[1]
     rows, width = features.shape
-    sub = rows // replicas // 2
+    subs = 2 * largest_divisor(rows // replicas // 32, SUBS // 2)
+    sub = rows // replicas // subs
     hops = blocks // 2
     vmem = pl.BlockSpec(memory_space=pltpu.VMEM)
     dma = pltpu.SemaphoreType.DMA
     return pl.pallas_call(
-        functools.partial(gather_kernel, blocks, replicas, sections),
-        out_shape=jax.ShapeDtypeStruct((sections, rows, width), features.dtype),
-        in_specs=[vmem],
-        out_specs=vmem,
+        functools.partial(gather_kernel, blocks, replicas, sections, subs),
+        out_shape=(
+            jax.ShapeDtypeStruct((sections, rows, width), features.dtype),
+            jax.ShapeDtypeStruct(tile_values.shape, tile_values.dtype),
+        ),
+        in_specs=[vmem, pl.BlockSpec(memory_space=pl.ANY)],
+        out_specs=(vmem, vmem),
         scratch_shapes=[
-            pltpu.VMEM((2, hops, 2, sub, width), features.dtype),
-            dma((2, hops, 2)), dma((2, hops, 2)), dma((2, hops, 2)), dma((sections, replicas, 2)), dma(()),
+            pltpu.VMEM((2, hops, subs, sub, width), features.dtype),
+            dma((2, hops, subs)), dma((2, hops, subs)), dma((2, hops, subs)),
+            dma((sections, replicas, subs)), dma(()), dma(()),
         ],
-        compiler_params=pltpu.CompilerParams(collective_id=1, has_side_effects=True),
+        compiler_params=pltpu.CompilerParams(collective_id=1, has_side_effects=True, vmem_limit_bytes=2 * GRANT),
+        cost_estimate=pl.CostEstimate(
+            flops=0, bytes_accessed=96 * rows * width * features.dtype.itemsize, transcendentals=0
+        ),
         name="gather_sources",
-    )(features)
+    )(features, tile_values)
 
 
 def sections_kernel(find, group, place_ref, count_ref, source_ref, tiles_ref, acc_ref):
@@ -152,18 +167,14 @@
         acc_ref[...] = jnp.zeros_like(acc_ref)
 
     def body(g, carry):
-        products, targets = [], []
         for u in range(group):
             k = g * group + u
             place = place_ref[0, section, base + k]
-            column = lax.rem(place, row_tiles)
-            targets.append(lax.div(place, row_tiles))
+            column, target = lax.rem(place, row_tiles), lax.div(place, row_tiles)
             piece = source_ref[section, pl.ds(pl.multiple_of(column * tile, tile), tile), :]
             product = jnp.dot(tiles_ref[0, 0, k], piece, preferred_element_type=jnp.float32)
-            products.append(jnp.where(base + k < count, product, 0.0))
-        for target, product in zip(targets, products):
             rows = pl.ds(pl.multiple_of(target * tile, tile), tile)
-            acc_ref[rows, :] += product
+            acc_ref[rows, :] += jnp.where(base + k < count, product, 0.0)
         return carry
 
     live = jnp.where(active, jnp.clip(count - base, 0, slots), 0)
@@ -199,6 +210,7 @@
             num_scalar_prefetch=2, grid=(sections * slots // block,),
             in_specs=[vmem, pl.BlockSpec((1, 1, block, tile, tile), tiles_map)], out_specs=vmem
         ),
+        compiler_params=pltpu.CompilerParams(vmem_limit_bytes=GRANT),
         name="section_sums",
     )(tile_place, tile_count, sources, tile_values)
 
@@ -300,17 +312,40 @@
             pltpu.VMEM((chips - 1, chunks, size, width), jnp.bfloat16),
             pltpu.VMEM((chips - 1, chunks, size, width), jnp.bfloat16),
         ] + [dma] * 8,
-        compiler_params=pltpu.CompilerParams(collective_id=0, has_side_effects=True),
+        compiler_params=pltpu.CompilerParams(collective_id=0, has_side_effects=True, vmem_limit_bytes=GRANT),
         name="replica_sum",
     )(part)
 
 
+def activate_kernel(agg_ref, weight_ref, bias_ref, out_ref):
+    output = jnp.dot(agg_ref[...], weight_ref[...], preferred_element_type=jnp.float32) + bias_ref[...]
+    out_ref[...] = jnp.maximum(output, 0.0).astype(out_ref.dtype)
+
+
+def activate(aggregated, weight, bias):
+    rows, width = aggregated.shape
+    hidden = weight.shape[1]
+    step = largest_divisor(rows, ROWS_STEP)
+    return pl.pallas_call(
+        activate_kernel,
+        out_shape=jax.ShapeDtypeStruct((rows, hidden), jnp.bfloat16),
+        grid=(rows // step,),
+        in_specs=[
+            pl.BlockSpec((step, width), lambda i: (i, 0)),
+            pl.BlockSpec((width, hidden), lambda i: (0, 0)),
+            pl.BlockSpec((1, hidden), lambda i: (0, 0)),
+        ],
+        out_specs=pl.BlockSpec((step, hidden), lambda i: (i, 0)),
+        compiler_params=pltpu.CompilerParams(vmem_limit_bytes=GRANT),
+        name="activate",
+    )(aggregated, weight, bias[None, :])
+
+
 def shards(blocks, replicas, features, weight, bias, tile_values, tile_place, tile_count):
-    sources = gather_sources(features, blocks, replicas, tile_values.shape[1])
-    part = section_sums(sources, tile_values, tile_place, tile_count)
+    sources, held = gather_sources(features, tile_values, blocks, replicas)
+    part = section_sums(sources, held, tile_place, tile_count)
     aggregated = replica_sum(part, replicas)
-    output = jnp.dot(aggregated, weight, preferred_element_type=jnp.float32) + bias
-    return jnp.maximum(output, 0.0).astype(jnp.bfloat16)
+    return activate(aggregated, weight, bias)
 
 
 def solution(mesh):

time: 71.2 us -> 60 us (0.84)
  the two profiles are of different devices: /device:TPU:27 before, /device:TPU:0 now
where the time goes in v3:
time: 60 us; the launch traced here: 59.4 us
  Pallas kernels  58 us (97%)
  local copies, waits for them, and re-layouts  1.24 us (2%)
    pallas_call x1, Pallas kernels, gather_sources(): pl.pallas_call(functools.partial(gather_kernel, blocks, replicas, section...  37 us
    pallas_call x1, Pallas kernels, replica_sum(): pl.pallas_call(functools.partial(reduce_kernel, chips, chunks), out_shape...  16 us
    pallas_call x1, Pallas kernels, section_sums(): pl.pallas_call(functools.partial(sections_kernel, find, group), out_shape...  3.07 us
    pallas_call x1, Pallas kernels, activate(): pl.pallas_call(activate_kernel, out_shape=jax.ShapeDtypeStruct((rows, hid...  2.01 us
    unnamed x10, local copies, waits for them, and re-layouts  1.24 us

profile of v3, /device:TPU:0, one launch (start us, length us, event | category | flops | bytes accessed | tf_op | source)
XLA Modules:
  0.0 59.4 jit_solution(7111980449838688645)
XLA Ops:
  0.0 0.0 copy-start
  0.0 1.2 %copy-done = bf16[4096,128]{1,0:T(8,128)(2,1)S(1)} copy-done((bf16[4096,128]{1,0:T(8,128)(2,1)S(1)}, bf16[4096,128]{1,0:T(8,128)(2,1)}, u32[]{:S(2)}) %copy-start) | copy-done | bytes 1048600
  1.2 0.0 copy-start.2
  1.2 0.0 copy-start.4
  1.2 37.0 %gather_sources.1 = (bf16[2,4096,128]{2,1,0:T(8,128)(2,1)S(1)}, bf16[1,2,160,128,128]{4,3,2,1,0:T(8,128)(2,1)S(1)}) custom-call(bf16[4096,128]{1,0:T(8,128)(2,1)S(1)} %copy-done, bf16[1,2,160,128,128]{4,3,2,1,0:T(8,128)(2,1)} %tiles_ref.1), custom_call_target="tpu_custom_call" | custom-call | bytes 100663296 | tf_op jit(solution)/shard_map/gather_sources/pallas_call | solution.py:136
  38.2 0.0 copy-done.2
  38.2 0.0 copy-done.4
  38.2 3.1 %section_sums.1.part_ref = f32[4096,128]{1,0:T(8,128)S(1)} custom-call(s32[1,2,160]{2,1,0:T(2,128)S(1)} %copy-done.2, s32[1,2]{1,0:T(1,128)S(1)} %copy-done.4, bf16[2,4096,128]{2,1,0:T(8,128)(2,1)S(1)} %get-tuple-element.7.source_ref, bf16[1,2,160,128,128]{4,3,2,1,0:T(8,128)(2,1)S(1)} %get-tuple-element.8.tiles_ref), custom_call_target="tpu_custom_call" | custom-call | tf_op jit(solution)/shard_map/section_sums/pallas_call | solution.py:206
  41.3 0.0 copy-start.1
  41.3 0.0 copy-start.3
  41.3 16.0 %replica_sum.1.agg_ref = bf16[4096,128]{1,0:T(8,128)(2,1)S(1)} custom-call(f32[4096,128]{1,0:T(8,128)S(1)} %section_sums.1.part_ref), custom_call_target="tpu_custom_call" | custom-call | tf_op jit(solution)/shard_map/replica_sum/pallas_call | solution.py:305
  57.3 0.0 copy-done.1
  57.3 0.0 copy-done.3
  57.4 2.0 %activate.1 = bf16[4096,256]{1,0:T(8,128)(2,1)} custom-call(bf16[4096,128]{1,0:T(8,128)(2,1)S(1)} %replica_sum.1.agg_ref, bf16[128,256]{1,0:T(8,128)(2,1)S(1)} %copy-done.1, f32[1,256]{1,0:T(1,128)S(1)} %bitcast.1), custom_call_target="tpu_custom_call" | custom-call | tf_op jit(solution)/shard_map/activate/pallas_call | solution.py:329
Async XLA Ops:
  0.0 1.2 %copy-start = (bf16[4096,128]{1,0:T(8,128)(2,1)S(1)}, bf16[4096,128]{1,0:T(8,128)(2,1)}, u32[]{:S(2)}) copy-start(bf16[4096,128]{1,0:T(8,128)(2,1)} %features_ref.1) | copy-start | bytes 3145732
  1.2 37.0 %copy-start.2 = (s32[1,2,160]{2,1,0:T(2,128)S(1)}, s32[1,2,160]{2,1,0:T(2,128)}, u32[]{:S(2)}) copy-start(s32[1,2,160]{2,1,0:T(2,128)} %place_ref.1) | copy-start | bytes 3844
  1.2 37.0 %copy-start.4 = (s32[1,2]{1,0:T(1,128)S(1)}, s32[1,2]{1,0:T(1,128)}, u32[]{:S(2)}) copy-start(s32[1,2]{1,0:T(1,128)} %count_ref.1) | copy-start | bytes 28
  41.3 16.0 %copy-start.1 = (bf16[128,256]{1,0:T(8,128)(2,1)S(1)}, bf16[128,256]{1,0:T(8,128)(2,1)}, u32[]{:S(2)}) copy-start(bf16[128,256]{1,0:T(8,128)(2,1)} %weight_ref.1) | copy-start | bytes 196612
  41.3 16.0 %copy-start.3 = (f32[256]{0:T(256)S(1)}, f32[256]{0:T(256)}, u32[]{:S(2)}) copy-start(f32[256]{0:T(256)} %param.8) | copy-start | bytes 3076
